TPU v7x, 128 devices: a whole 4x4x4 slice. The times are simulated.
128 devices in a mesh: ctx: 16 (over y_hi, x, core), vocab: 8 (over y_lo, z).
Axes of the slice: x: 4, y: 4 (y_hi: 2, y_lo: 2; y = y_hi * 2 + y_lo), z: 4, core: 2. Of those that a mesh axis runs over, the one named last changes fastest.
Arguments:
- block_query: bfloat16 [512, 6144], P('ctx', 'vocab'), may hold values from -16 to 16
- block_key: bfloat16 [512, 6144], P('ctx', 'vocab'), may hold values from -16 to 16
- block_value: bfloat16 [512, 6144], P('ctx', 'vocab'), may hold values from -6 to 6
- block_doc: int32 [512], P('ctx'), may hold values from 0 to 1, never falling along the last dimension, each value on 1 to 480 neighbouring positions
- token_query: bfloat16 [2048, 6144], P(('ctx', 'vocab')), may hold values from -16 to 16
- token_key: bfloat16 [2048, 6144], P(('ctx', 'vocab')), may hold values from -16 to 16
- token_value: bfloat16 [2048, 6144], P(('ctx', 'vocab')), may hold values from -600 to 600
- token_state: bfloat16 [2048, 6144], P(('ctx', 'vocab')), may hold values from -6 to 6
- norm_gain: float32 [6144], replicated, may hold values from 0.5 to 1.5
- head_weight: bfloat16 [6144, 131072], P(None, ('ctx', 'vocab')), may hold values from -128 to 128
- targets: int32 [2048], replicated, may hold values from 0 to 131071
Outputs:
- block_context: bfloat16 [512, 6144], P('ctx', 'vocab')
- token_prior: float32 [2048], P(('ctx', 'vocab'))
Inputs may be any that keep to these rules, and one draw needn't show every extreme that they name: block_doc never falls along the blocks; no document holds more than 480 blocks.
All inputs are finite; a program needn't handle non-finite values.
Results may differ from a plain program's by a relative error of at most 0.005.
Values may be sent and summed in bfloat16 or wider, within the bound.
No kernel may reach another device: no remote copies, remote signals or barrier semaphores. Data moves between devices by JAX's collectives and lax.ppermute only.
A program may use at most 128 MiB of HBM per device.

v0:
```python
import math
import jax
import jax.numpy as jnp
from jax import lax
from jax.sharding import Mesh
from jax.sharding import PartitionSpec as P

HEAD_DIM = 128
BLOCK_LEN = 4
CTX = ("ctx_0", "ctx_1", "ctx_2")
VOCAB = ("vocab_0", "vocab_1")
CTX_VOCAB = ("ctx_0", "ctx_1", "ctx_2", "vocab_0", "vocab_1")
big_negative = -1e30


def sent_to_all(value, axis):
    size = lax.axis_size(axis)
    return lax.all_to_all(
        jnp.broadcast_to(value[None], (size, *value.shape)), axis, 0, 0, tiled=True
    )


def joined_along(pieces, dim):
    pieces = jnp.moveaxis(pieces, 0, dim)
    shape = pieces.shape
    return pieces.reshape(*shape[:dim], shape[dim] * shape[dim + 1], *shape[dim + 2 :])


def gathered_copies(value, axis, dim):
    pieces = sent_to_all(value, axis)
    return joined_along(pieces, dim)


def all_in_one(value, axis):
    leaves = jax.tree.leaves(value)
    sequence = sorted(range(len(leaves)), key=lambda k: -leaves[k].size)
    width = (1, *leaves[sequence[0]].shape)[-1]
    lines = [
        jnp.pad(leaves[k].reshape(-1), (0, -leaves[k].size % width)).reshape(-1, width)
        for k in sequence
    ]
    both, at, found = (lax.all_gather(jnp.concatenate(lines), axis), 0, {})
    for k, line in zip(sequence, lines):
        share = both[:, at : at + len(line)].reshape(len(both), -1)
        found[k] = share[:, : leaves[k].size].reshape(-1, *leaves[k].shape)
        at += len(line)
    numbers = iter(range(len(leaves)))
    return jax.tree.map(lambda _: found[next(numbers)], value)


def merged_by_axis(value, axes, combine):
    for axis in axes:
        pieces = all_in_one(value, axis)
        value = jax.tree.map(lambda part: part[0], pieces)
        for k in range(1, lax.axis_size(axis)):
            value = combine(value, jax.tree.map(lambda part: part[k], pieces))
    return value


def local_decoder(context, token_query, token_key, token_value, token_state, norm_gain):
    scale = 1.0 / math.sqrt(HEAD_DIM)
    groups = context.shape[0]
    width = context.shape[1]
    head_total = width // HEAD_DIM
    shape = (groups, BLOCK_LEN, head_total, HEAD_DIM)
    prefix = context.reshape(groups, 1, head_total, HEAD_DIM)
    queries = token_query.reshape(shape)
    keys = jnp.concatenate([prefix, token_key.reshape(shape)], axis=1)
    values = jnp.concatenate([prefix, token_value.reshape(shape)], axis=1)
    scores = (
        jnp.einsum("bihd,bjhd->bhij", queries, keys, preferred_element_type=jnp.float32) * scale
    )
    allowed = (
        jnp.arange(BLOCK_LEN + 1, dtype=jnp.int32)[None, :]
        <= jnp.arange(BLOCK_LEN, dtype=jnp.int32)[:, None] + 1
    )
    scores = jnp.where(allowed, scores, -jnp.inf)
    highest = jnp.max(scores, axis=-1, keepdims=True)
    weights = jnp.exp(scores - highest)
    totals = jnp.sum(weights, axis=-1)
    mixed = jnp.einsum(
        "bhij,bjhd->bihd", weights.astype(jnp.bfloat16), values, preferred_element_type=jnp.float32
    )
    mixed = mixed / jnp.transpose(totals, (0, 2, 1))[..., None]
    summed = token_state.astype(jnp.float32) + mixed.reshape(groups * BLOCK_LEN, width)
    power = jnp.mean(summed * summed, axis=-1, keepdims=True)
    return (summed * lax.rsqrt(power + 1e-05) * norm_gain).astype(jnp.bfloat16)


def local(
    block_query,
    block_key,
    block_value,
    block_doc,
    token_query,
    token_key,
    token_value,
    token_state,
    norm_gain,
    head_weight,
    targets,
):
    local_rows = block_query.shape[0]
    head_count = block_query.shape[1] // HEAD_DIM
    scale = 1.0 / math.sqrt(HEAD_DIM)
    first_row = lax.axis_index(CTX) * local_rows
    queries = block_query.reshape(local_rows, head_count, HEAD_DIM)
    own_doc = block_doc.astype(jnp.bfloat16)
    query_places = first_row + jnp.arange(local_rows, dtype=jnp.int32)
    highest = jnp.full((local_rows, head_count), big_negative, jnp.float32)
    keys = lax.all_gather(block_key, CTX, axis=0, tiled=True)
    values = lax.all_gather(block_value, CTX, axis=0, tiled=True)
    docs = lax.all_gather(own_doc, CTX, axis=0, tiled=True)
    count = keys.shape[0]
    keys = keys.reshape(count, head_count, HEAD_DIM)
    values = values.reshape(count, head_count, HEAD_DIM)
    scores = jnp.einsum("qhd,khd->qhk", queries, keys, preferred_element_type=jnp.float32) * scale
    key_places = jnp.arange(count, dtype=jnp.int32)
    allowed = (query_places[:, None] >= key_places[None, :]) & (own_doc[:, None] == docs[None, :])
    allowed = allowed[:, None, :]
    newest = jnp.maximum(highest, jnp.max(jnp.where(allowed, scores, big_negative), axis=-1))
    weights = jnp.where(allowed, jnp.exp(scores - newest[..., None]), 0.0)
    totals = jnp.sum(weights, axis=-1)
    update = jnp.einsum(
        "qhk,khd->qhd", weights.astype(jnp.bfloat16), values, preferred_element_type=jnp.float32
    )
    mixed = update
    highest, totals, mixed = (newest, totals, mixed)
    block_context = (
        (mixed / totals[..., None]).reshape(local_rows, head_count * HEAD_DIM).astype(jnp.bfloat16)
    )
    grouped = lax.all_to_all(block_context, VOCAB, split_axis=0, concat_axis=1, tiled=True)
    hidden = local_decoder(grouped, token_query, token_key, token_value, token_state, norm_gain)
    vocab_cols = head_weight.shape[1]
    col_start = lax.axis_index(CTX_VOCAB) * vocab_cols
    columns = jnp.arange(vocab_cols, dtype=jnp.int32)
    group_states = gathered_copies(hidden, VOCAB, 0)
    piece = lax.all_gather(group_states, CTX, axis=0, tiled=True)
    logits = jnp.dot(piece, head_weight, preferred_element_type=jnp.float32)
    top = jnp.max(logits, axis=-1)
    mass = jnp.sum(jnp.exp(logits - top[:, None]), axis=-1)
    wanted = targets - col_start
    picked = jnp.sum(jnp.where(columns[None, :] == wanted[:, None], logits, 0.0), axis=1)
    peaks = top
    masses = mass
    picks = picked
    stats = (peaks, masses, picks)

    def combine(left, right):
        top = jnp.maximum(left[0], right[0])
        mass = left[1] * jnp.exp(left[0] - top) + right[1] * jnp.exp(right[0] - top)
        return (top, mass, left[2] + right[2])

    peaks, masses, picks = merged_by_axis(stats, CTX_VOCAB, combine)
    priors = picks - (peaks + jnp.log(masses))
    own_count = hidden.shape[0]
    token_prior = lax.dynamic_slice_in_dim(priors, lax.axis_index(CTX_VOCAB) * own_count, own_count)
    return (block_context, token_prior)


def solution(mesh):
    torus = Mesh(
        mesh.devices.reshape(2, 4, 2, 2, 4), ("ctx_0", "ctx_1", "ctx_2", "vocab_0", "vocab_1")
    )
    in_specs = (
        P(CTX, VOCAB),
        P(CTX, VOCAB),
        P(CTX, VOCAB),
        P(CTX),
        P(CTX_VOCAB, None),
        P(CTX_VOCAB, None),
        P(CTX_VOCAB, None),
        P(CTX_VOCAB, None),
        P(),
        P(None, CTX_VOCAB),
        P(),
    )
    out_specs = (P(CTX, VOCAB), P(CTX_VOCAB))
    return jax.shard_map(local, mesh=torus, in_specs=in_specs, out_specs=out_specs, check_vma=False)
```

profile of v0, /device:TPU:0, one launch (start us, length us, event | category | flops | bytes accessed | tf_op | source)
XLA Modules:
  0.0 360.8 jit_solution(2283637337288649313)
XLA Ops:
  7.2 0.0 copy-start
  7.2 0.0 copy-start.2
  7.2 0.0 copy-start.3
  7.2 0.8 convert_element_type.25
  8.0 1.2 dynamic-slice
  9.9 0.2 dynamic-update-slice
  10.1 38.1 %all-reduce = bf16[512]{0:T(512)(128)(2,1)S(1)} all-reduce(bf16[512]{0:T(512)(128)(2,1)S(1)} %dynamic-update-slice), channel_id=1, replica_groups=mesh['ctx_0'=2,'ctx_1'=4,'ctx_2'=2,'vocab_0'=2,'vocab_1'=4] {'ctx_0','ct..., use_global_device_ids=true, to_apply=%add | all-reduce | flops 512 | bytes 2048
  48.2 21.7 %all_gather.43 = bf16[512,768]{1,0:T(8,128)(2,1)S(1)} all-gather(bf16[32,768]{1,0:T(8,128)(2,1)} %param.12), channel_id=1, replica_groups=mesh['ctx_0'=2,'ctx_1'=4,'ctx_2'=2,'vocab_0'=2,'vocab_1'=4] {'ctx_0','ct..., dimensions={0}, use_global_device_ids=true | all-gather | bytes 835584 | tf_op jit(solution)/shard_map/all_gather | solution.py:111
  69.9 0.0 copy-start.1
  69.9 0.3 copy.29
  70.2 0.0 copy-start.4
  70.2 0.1 fusion.19
  70.3 0.0 copy-done
  70.3 0.3 select_reduce_fusion.1
  70.6 23.0 %all_gather.44 = bf16[512,768]{1,0:T(8,128)(2,1)S(1)} all-gather(bf16[32,768]{1,0:T(8,128)(2,1)} %param.13), channel_id=1, replica_groups=mesh['ctx_0'=2,'ctx_1'=4,'ctx_2'=2,'vocab_0'=2,'vocab_1'=4] {'ctx_0','ct..., dimensions={0}, use_global_device_ids=true | all-gather | bytes 835584 | tf_op jit(solution)/shard_map/all_gather | solution.py:112
  93.6 0.3 copy.32
  93.9 0.2 fusion.8
  94.1 0.4 fusion.5
  94.6 0.7 convert_element_type.30
  95.2 5.4 %all-to-all-start = ((bf16[8,4,768]{2,1,0:T(4,128)(2,1)}), bf16[8,4,768]{2,1,0:T(4,128)(2,1)S(1)}, u32[]{:S(2)}, u32[]{:S(2)}) async-start(bf16[8,4,768]{2,1,0:T(4,128)(2,1)} %convert_element_type.30), calls=%async_computation | async-start | bytes 98304 | tf_op jit(solution)/shard_map/all_to_all | solution.py:132
  100.6 0.0 all-gather.12.cloned.1.call-start
  100.7 0.1 iota_compare_fusion.2
  100.8 1.0 copy.48
  101.7 0.1 copy.40
  101.8 0.0 copy-done.2
  101.9 0.0 copy-start.5
  101.9 0.0 copy-done.3
  101.9 0.1 copy.38
  102.0 4.9 %all-to-all-done = bf16[8,4,768]{2,1,0:T(4,128)(2,1)S(1)} async-done(((bf16[8,4,768]{2,1,0:T(4,128)(2,1)}), bf16[8,4,768]{2,1,0:T(4,128)(2,1)S(1)}, u32[]{:S(2)}, u32[]{:S(2)}) %all-to-all-start) | async-done | bytes 49184 | tf_op jit(solution)/shard_map/all_to_all | solution.py:132
  107.0 0.5 fusion.61
  107.5 0.5 fusion.10
  108.0 0.6 fusion
  108.6 0.0 copy-done.1
  108.6 0.2 multiply_reduce_fusion
  108.9 0.0 copy-done.4
  108.9 0.2 multiply_convert_fusion
  109.0 0.1 broadcast_in_dim.61
  109.2 23.8 %all_to_all.18 = bf16[8,16,6144]{2,1,0:T(8,128)(2,1)} all-to-all(bf16[8,16,6144]{2,1,0:T(8,128)(2,1)S(1)} %broadcast_in_dim.61), channel_id=1, replica_groups=mesh['ctx_0'=2,'ctx_1'=4,'ctx_2'=2,'vocab_0'=2,'vocab_1'=4] {'vocab_0','..., dimensions={0} | all-to-all | bytes 3145728 | tf_op jit(solution)/shard_map/all_to_all | solution.py:18
  133.0 0.0 all-gather.12.cloned.1.call-update
  133.1 0.0 copy-done.5
  133.1 0.6 copy_bitcast_fusion
  133.7 143.4 %all-gather.12.cloned.1.call-done = bf16[2048,6144]{1,0:T(8,128)(2,1)} async-done(((bf16[128,6144]{1,0:T(8,128)(2,1)}), bf16[2048,6144]{1,0:T(8,128)(2,1)}) %all-gather.12.cloned.1.call-update) | async-done | bytes 25165840 | tf_op jit(solution)/shard_map/all_gather | solution.py:138
  277.1 34.1 %fusion.62 = (f32[2048]{0:T(1024)S(1)}, f32[2048,1024]{0,1:T(8,128)}) fusion(bf16[2048,6144]{1,0:T(8,128)(2,1)} %all-gather.12.cloned.1.call-done, bf16[6144,1024]{1,0:T(8,128)(2,1)} %param.20), kind=kOutput, calls=%fused_computation.121 | convolution fusion | flops 25771898880 | bytes 46145536 | tf_op jit(solution)/shard_map/dot_general | solution.py:139
  311.2 4.6 %exponential_reduce_fusion = (f32[2048]{0:T(1024)S(1)}, f32[2048]{0:T(1024)S(1)}) fusion(f32[2048,1024]{0,1:T(8,128)} %get-tuple-element.31, f32[2048]{0:T(1024)S(1)} %get-tuple-element.30, s32[2048]{0:T(1024)S(1)} %broadcast_subtract_fusion), kind=kLoop, calls=%fused_computation.2 | loop fusion | flops 10481664 | bytes 8421376 | tf_op jit(solution)/shard_map/reduce_sum | solution.py:141
  315.8 6.1 %all-gather.5 = f32[2,3,2048]{2,1,0:T(4,128)S(1)} all-gather(f32[1,3,2048]{2,1,0:T(4,128)S(1)} %maximum_bitcast_fusion), channel_id=2, replica_groups=mesh['ctx_0'=2,'ctx_1'=4,'ctx_2'=2,'vocab_0'=2,'vocab_1'=4] {'ctx_0'}, dimensions={0}, use_global_device_ids=true | all-gather | bytes 73728 | tf_op jit(solution)/shard_map/all_gather | solution.py:42
  322.0 12.0 %all-gather.6 = f32[4,3,2048]{2,1,0:T(4,128)S(1)} all-gather(f32[1,3,2048]{2,1,0:T(4,128)S(1)} %maximum_bitcast_fusion.1), channel_id=3, replica_groups=mesh['ctx_0'=2,'ctx_1'=4,'ctx_2'=2,'vocab_0'=2,'vocab_1'=4] {'ctx_1'}, dimensions={0}, use_global_device_ids=true | all-gather | bytes 122880 | tf_op jit(solution)/shard_map/all_gather | solution.py:42
  334.0 0.1 fusion.32
  334.2 1.9 all-gather.7
  336.1 4.6 %all-gather.8 = f32[2,3,2048]{2,1,0:T(4,128)S(1)} all-gather(f32[1,3,2048]{2,1,0:T(4,128)S(1)} %maximum_bitcast_fusion.3), channel_id=5, replica_groups=mesh['ctx_0'=2,'ctx_1'=4,'ctx_2'=2,'vocab_0'=2,'vocab_1'=4] {'vocab_0'}, dimensions={0}, use_global_device_ids=true | all-gather | bytes 73728 | tf_op jit(solution)/shard_map/all_gather | solution.py:42
  340.8 12.5 %all-gather.9 = f32[4,3,2048]{2,1,0:T(4,128)S(1)} all-gather(f32[1,3,2048]{2,1,0:T(4,128)S(1)} %maximum_bitcast_fusion.4), channel_id=6, replica_groups=mesh['ctx_0'=2,'ctx_1'=4,'ctx_2'=2,'vocab_0'=2,'vocab_1'=4] {'vocab_1'}, dimensions={0}, use_global_device_ids=true | all-gather | bytes 122880 | tf_op jit(solution)/shard_map/all_gather | solution.py:42
  353.3 0.1 fusion.60
  353.4 0.6 dynamic-slice_subtract_fusion
  (27 shorter events, 0.5 us)
Async XLA Ops:
  7.2 63.1 %copy-start = (bf16[32,768]{1,0:T(8,128)(2,1)S(1)}, bf16[32,768]{1,0:T(8,128)(2,1)}, u32[]{:S(2)}) copy-start(bf16[32,768]{1,0:T(8,128)(2,1)} %param.11) | copy-start | bytes 147460
  7.2 94.6 %copy-start.2 = (bf16[16,6144]{1,0:T(8,128)(2,1)S(1)}, bf16[16,6144]{1,0:T(8,128)(2,1)}, u32[]{:S(2)}) copy-start(bf16[16,6144]{1,0:T(8,128)(2,1)} %param.15) | copy-start | bytes 589828
  7.2 94.7 %copy-start.3 = (bf16[16,6144]{1,0:T(8,128)(2,1)S(1)}, bf16[16,6144]{1,0:T(8,128)(2,1)}, u32[]{:S(2)}) copy-start(bf16[16,6144]{1,0:T(8,128)(2,1)} %param.17) | copy-start | bytes 589828
  69.9 38.7 %copy-start.1 = (bf16[16,6144]{1,0:T(8,128)(2,1)S(1)}, bf16[16,6144]{1,0:T(8,128)(2,1)}, u32[]{:S(2)}) copy-start(bf16[16,6144]{1,0:T(8,128)(2,1)} %param.18) | copy-start | bytes 589828
  70.2 38.7 %copy-start.4 = (f32[6144]{0:T(1024)S(1)}, f32[6144]{0:T(1024)}, u32[]{:S(2)}) copy-start(f32[6144]{0:T(1024)} %param.19) | copy-start | bytes 73732
  95.2 11.7 %all-to-all-start = ((bf16[8,4,768]{2,1,0:T(4,128)(2,1)}), bf16[8,4,768]{2,1,0:T(4,128)(2,1)S(1)}, u32[]{:S(2)}, u32[]{:S(2)}) async-start(bf16[8,4,768]{2,1,0:T(4,128)(2,1)} %convert_element_type.30), calls=%async_computation | async-start | bytes 98304 | tf_op jit(solution)/shard_map/all_to_all | solution.py:132
  100.6 176.4 %all-gather.12.cloned.1.call-start = ((), (), s32[]{:S(2)}) async-start(), calls=%async_computation.2 | async-start | bytes 26738688 | tf_op jit(solution)/shard_map/all_gather | solution.py:138
  101.9 31.2 %copy-start.5 = (s32[2048]{0:T(1024)S(1)}, s32[2048]{0:T(1024)}, u32[]{:S(2)}) copy-start(s32[2048]{0:T(1024)} %param.21) | copy-start | bytes 24580
Sparse Core Ops, SparseCore 0:
  133.2 143.8 all-gather.11
where the time goes:
time: 361 us
  waiting for transfers between devices  148 us (41%)
  blocking collectives  144 us (40%)
  matrix products  35.9 us (10%)
  between operations  15.1 us (4%)
  other arithmetic  7.79 us (2%)
  starting transfers between devices  5.47 us (2%)
  local copies, waits for them, and re-layouts  4.76 us (1%)
    all_gather x1, waiting for transfers between devices, local(): piece = lax.all_gather(group_states, CTX, axis=0, tiled=True)  143 us
    unnamed x1, blocking collectives  38.1 us
    all_gather x5, blocking collectives, all_in_one(): both, at, found = (lax.all_gather(jnp.concatenate(lines), axis), 0, {})  37 us
    dot_general x1, matrix products, local(): logits = jnp.dot(piece, head_weight, preferred_element_type=jnp.float32)  34.1 us
    all_to_all x1, blocking collectives, sent_to_all(): lax.all_to_all(jnp.broadcast_to(value[None], (size, *value.shape)), axis,...  23.8 us
    all_gather x1, blocking collectives, local(): values = lax.all_gather(block_value, CTX, axis=0, tiled=True)  23 us
    all_gather x1, blocking collectives, local(): keys = lax.all_gather(block_key, CTX, axis=0, tiled=True)  21.7 us
  transfers between devices with their start and end apart: 2, of which 2 were waited for; matrix products, arithmetic and copies ran while one was open for 1% of the time, Pallas kernels for 0%

commit v1 on v0

--- a/solution.py
+++ b/solution.py
@@ -109,7 +109,9 @@
     query_places = first_row + jnp.arange(local_rows, dtype=jnp.int32)
     highest = jnp.full((local_rows, head_count), big_negative, jnp.float32)
     keys = lax.all_gather(block_key, CTX, axis=0, tiled=True)
-    values = lax.all_gather(block_value, CTX, axis=0, tiled=True)
+    values = jnp.concatenate(
+        lax.all_to_all(jnp.stack([block_value] * lax.axis_size(CTX)), CTX, 0, 0), axis=0
+    )
     docs = lax.all_gather(own_doc, CTX, axis=0, tiled=True)
     count = keys.shape[0]
     keys = keys.reshape(count, head_count, HEAD_DIM)

time: 361 us -> 350 us (0.970)
  blocking collectives: 144 us -> 121 us
  starting transfers between devices: 5.47 us -> 12.6 us
    all_gather x1 -> x0, blocking collectives: 23 us -> none  [local(): values = lax.all_gather(block_value, CTX, axis=0, tiled=True)]
    all_to_all x0 -> x1, starting transfers between devices: none -> 7.15 us  [local(): lax.all_to_all(jnp.stack([block_value] * lax.axis_size(CTX)), CTX, 0, 0)]
  transfers between devices with their start and end apart: 2 -> 3, of which waited for: 2 -> 2; matrix products, arithmetic and copies ran while one was open for 1% -> 1% of each run, Pallas kernels for 0% -> 0%
where the time goes in v1:
time: 350 us; the launch traced here: 349 us
  waiting for transfers between devices  151 us (43%)
  blocking collectives  121 us (35%)
  matrix products  35.8 us (10%)
  between operations  15.1 us (4%)
  starting transfers between devices  12.6 us (4%)
  other arithmetic  7.72 us (2%)
  local copies, waits for them, and re-layouts  6.26 us (2%)
    all_gather x1, waiting for transfers between devices, local(): piece = lax.all_gather(group_states, CTX, axis=0, tiled=True)  145 us
    unnamed x1, blocking collectives  38.4 us
    all_gather x5, blocking collectives, all_in_one(): both, at, found = (lax.all_gather(jnp.concatenate(lines), axis), 0, {})  37 us
    dot_general x1, matrix products, local(): logits = jnp.dot(piece, head_weight, preferred_element_type=jnp.float32)  34.1 us
    all_to_all x1, blocking collectives, sent_to_all(): lax.all_to_all(jnp.broadcast_to(value[None], (size, *value.shape)), axis,...  23.8 us
    all_gather x1, blocking collectives, local(): keys = lax.all_gather(block_key, CTX, axis=0, tiled=True)  21.7 us
    all_to_all x1, starting transfers between devices, local(): lax.all_to_all(jnp.stack([block_value] * lax.axis_size(CTX)), CTX, 0, 0)  7.15 us
  transfers between devices with their start and end apart: 3, of which 2 were waited for; matrix products, arithmetic and copies ran while one was open for 1% of the time, Pallas kernels for 0%

profile of v1, /device:TPU:0, one launch (start us, length us, event | category | flops | bytes accessed | tf_op | source)
XLA Modules:
  0.0 349.3 jit_solution(6851544545165855082)
XLA Ops:
  7.2 0.0 copy-start
  7.2 0.0 copy-start.2
  7.2 0.0 copy-start.3
  7.2 0.0 copy-start.4
  7.2 1.8 stack.2
  9.0 7.1 %all-to-all-start = ((bf16[16,32,768]{2,1,0:T(8,128)(2,1)}), bf16[16,32,768]{2,1,0:T(8,128)(2,1)S(1)}, u32[]{:S(2)}, u32[]{:S(2)}) async-start(bf16[16,32,768]{2,1,0:T(8,128)(2,1)} %stack.2), calls=%async_computation | async-start | bytes 1572864 | tf_op jit(solution)/shard_map/all_to_all | solution.py:113
  16.2 0.7 convert_element_type.25
  16.9 1.2 dynamic-slice
  18.8 0.2 dynamic-update-slice
  19.0 38.4 %all-reduce = bf16[512]{0:T(512)(128)(2,1)S(1)} all-reduce(bf16[512]{0:T(512)(128)(2,1)S(1)} %dynamic-update-slice), channel_id=1, replica_groups=mesh['ctx_0'=2,'ctx_1'=4,'ctx_2'=2,'vocab_0'=2,'vocab_1'=4] {'ctx_0','ct..., use_global_device_ids=true, to_apply=%add | all-reduce | flops 512 | bytes 2048
  57.4 21.7 %all_gather.40 = bf16[512,768]{1,0:T(8,128)(2,1)S(1)} all-gather(bf16[32,768]{1,0:T(8,128)(2,1)} %param.12), channel_id=1, replica_groups=mesh['ctx_0'=2,'ctx_1'=4,'ctx_2'=2,'vocab_0'=2,'vocab_1'=4] {'ctx_0','ct..., dimensions={0}, use_global_device_ids=true | all-gather | bytes 835584 | tf_op jit(solution)/shard_map/all_gather | solution.py:111
  79.1 0.1 fusion.20
  79.2 0.0 copy-start.1
  79.2 0.3 copy.28
  79.5 0.0 copy-start.5
  79.5 0.0 copy-done
  79.5 0.3 select_reduce_fusion.1
  79.8 0.2 fusion.9
  80.1 0.0 all-to-all-done
  80.1 0.9 reshape_reshape.3
  81.0 0.3 fusion.5
  81.3 0.7 convert_element_type.30
  82.0 5.4 %all-to-all-start.1 = ((bf16[8,4,768]{2,1,0:T(4,128)(2,1)}), bf16[8,4,768]{2,1,0:T(4,128)(2,1)S(1)}, u32[]{:S(2)}, u32[]{:S(2)}) async-start(bf16[8,4,768]{2,1,0:T(4,128)(2,1)} %convert_element_type.30), calls=%async_computation.1 | async-start | bytes 98304 | tf_op jit(solution)/shard_map/all_to_all | solution.py:134
  87.4 0.0 all-gather.12.cloned.1.call-start
  87.5 0.1 iota_compare_fusion.2
  87.5 0.0 copy-done.2
  87.6 0.1 copy.38
  87.7 0.0 copy-done.3
  87.7 0.0 copy-start.6
  87.7 0.0 copy-done.4
  87.8 0.1 copy.36
  87.9 5.9 %all-to-all-done.1 = bf16[8,4,768]{2,1,0:T(4,128)(2,1)S(1)} async-done(((bf16[8,4,768]{2,1,0:T(4,128)(2,1)}), bf16[8,4,768]{2,1,0:T(4,128)(2,1)S(1)}, u32[]{:S(2)}, u32[]{:S(2)}) %all-to-all-start.1) | async-done | bytes 49184 | tf_op jit(solution)/shard_map/all_to_all | solution.py:134
  93.8 0.5 fusion.62
  94.3 0.5 fusion.11
  94.8 0.6 fusion
  95.4 0.0 copy-done.1
  95.4 0.2 multiply_reduce_fusion
  95.6 0.0 copy-done.5
  95.7 0.2 multiply_convert_fusion
  95.8 0.1 broadcast_in_dim.61
  96.0 23.8 %all_to_all.23 = bf16[8,16,6144]{2,1,0:T(8,128)(2,1)} all-to-all(bf16[8,16,6144]{2,1,0:T(8,128)(2,1)S(1)} %broadcast_in_dim.61), channel_id=1, replica_groups=mesh['ctx_0'=2,'ctx_1'=4,'ctx_2'=2,'vocab_0'=2,'vocab_1'=4] {'vocab_0','..., dimensions={0} | all-to-all | bytes 3145728 | tf_op jit(solution)/shard_map/all_to_all | solution.py:18
  119.8 0.0 all-gather.12.cloned.1.call-update
  119.9 0.0 copy-done.6
  119.9 0.6 copy_bitcast_fusion
  120.5 145.1 %all-gather.12.cloned.1.call-done = bf16[2048,6144]{1,0:T(8,128)(2,1)} async-done(((bf16[128,6144]{1,0:T(8,128)(2,1)}), bf16[2048,6144]{1,0:T(8,128)(2,1)}) %all-gather.12.cloned.1.call-update) | async-done | bytes 25165840 | tf_op jit(solution)/shard_map/all_gather | solution.py:140
  265.6 34.1 %fusion.63 = (f32[2048]{0:T(1024)S(1)}, f32[2048,1024]{0,1:T(8,128)}) fusion(bf16[2048,6144]{1,0:T(8,128)(2,1)} %all-gather.12.cloned.1.call-done, bf16[6144,1024]{1,0:T(8,128)(2,1)} %param.20), kind=kOutput, calls=%fused_computation.122 | convolution fusion | flops 25771898880 | bytes 46145536 | tf_op jit(solution)/shard_map/dot_general | solution.py:141
  299.7 4.6 %exponential_reduce_fusion = (f32[2048]{0:T(1024)S(1)}, f32[2048]{0:T(1024)S(1)}) fusion(f32[2048,1024]{0,1:T(8,128)} %get-tuple-element.31, f32[2048]{0:T(1024)S(1)} %get-tuple-element.30, s32[2048]{0:T(1024)S(1)} %broadcast_subtract_fusion), kind=kLoop, calls=%fused_computation.2 | loop fusion | flops 10481664 | bytes 8421376 | tf_op jit(solution)/shard_map/reduce_sum | solution.py:143
  304.3 6.1 %all-gather.5 = f32[2,3,2048]{2,1,0:T(4,128)S(1)} all-gather(f32[1,3,2048]{2,1,0:T(4,128)S(1)} %maximum_bitcast_fusion), channel_id=2, replica_groups=mesh['ctx_0'=2,'ctx_1'=4,'ctx_2'=2,'vocab_0'=2,'vocab_1'=4] {'ctx_0'}, dimensions={0}, use_global_device_ids=true | all-gather | bytes 73728 | tf_op jit(solution)/shard_map/all_gather | solution.py:42
  310.5 12.0 %all-gather.6 = f32[4,3,2048]{2,1,0:T(4,128)S(1)} all-gather(f32[1,3,2048]{2,1,0:T(4,128)S(1)} %maximum_bitcast_fusion.1), channel_id=3, replica_groups=mesh['ctx_0'=2,'ctx_1'=4,'ctx_2'=2,'vocab_0'=2,'vocab_1'=4] {'ctx_1'}, dimensions={0}, use_global_device_ids=true | all-gather | bytes 122880 | tf_op jit(solution)/shard_map/all_gather | solution.py:42
  322.5 0.1 fusion.33
  322.7 1.9 all-gather.7
  324.6 4.6 %all-gather.8 = f32[2,3,2048]{2,1,0:T(4,128)S(1)} all-gather(f32[1,3,2048]{2,1,0:T(4,128)S(1)} %maximum_bitcast_fusion.3), channel_id=5, replica_groups=mesh['ctx_0'=2,'ctx_1'=4,'ctx_2'=2,'vocab_0'=2,'vocab_1'=4] {'vocab_0'}, dimensions={0}, use_global_device_ids=true | all-gather | bytes 73728 | tf_op jit(solution)/shard_map/all_gather | solution.py:42
  329.3 12.5 %all-gather.9 = f32[4,3,2048]{2,1,0:T(4,128)S(1)} all-gather(f32[1,3,2048]{2,1,0:T(4,128)S(1)} %maximum_bitcast_fusion.4), channel_id=6, replica_groups=mesh['ctx_0'=2,'ctx_1'=4,'ctx_2'=2,'vocab_0'=2,'vocab_1'=4] {'vocab_1'}, dimensions={0}, use_global_device_ids=true | all-gather | bytes 122880 | tf_op jit(solution)/shard_map/all_gather | solution.py:42
  341.8 0.1 fusion.61
  341.9 0.6 dynamic-slice_subtract_fusion
  (28 shorter events, 0.6 us)
Async XLA Ops:
  7.2 72.3 %copy-start = (bf16[32,768]{1,0:T(8,128)(2,1)S(1)}, bf16[32,768]{1,0:T(8,128)(2,1)}, u32[]{:S(2)}) copy-start(bf16[32,768]{1,0:T(8,128)(2,1)} %param.11) | copy-start | bytes 147460
  7.2 80.4 %copy-start.2 = (bf16[16,6144]{1,0:T(8,128)(2,1)S(1)}, bf16[16,6144]{1,0:T(8,128)(2,1)}, u32[]{:S(2)}) copy-start(bf16[16,6144]{1,0:T(8,128)(2,1)} %param.16) | copy-start | bytes 589828
  7.2 80.5 %copy-start.3 = (bf16[16,6144]{1,0:T(8,128)(2,1)S(1)}, bf16[16,6144]{1,0:T(8,128)(2,1)}, u32[]{:S(2)}) copy-start(bf16[16,6144]{1,0:T(8,128)(2,1)} %param.15) | copy-start | bytes 589828
  7.2 80.5 %copy-start.4 = (bf16[16,6144]{1,0:T(8,128)(2,1)S(1)}, bf16[16,6144]{1,0:T(8,128)(2,1)}, u32[]{:S(2)}) copy-start(bf16[16,6144]{1,0:T(8,128)(2,1)} %param.17) | copy-start | bytes 589828
  9.0 71.0 %all-to-all-start = ((bf16[16,32,768]{2,1,0:T(8,128)(2,1)}), bf16[16,32,768]{2,1,0:T(8,128)(2,1)S(1)}, u32[]{:S(2)}, u32[]{:S(2)}) async-start(bf16[16,32,768]{2,1,0:T(8,128)(2,1)} %stack.2), calls=%async_computation | async-start | bytes 1572864 | tf_op jit(solution)/shard_map/all_to_all | solution.py:113
  79.2 16.2 %copy-start.1 = (bf16[16,6144]{1,0:T(8,128)(2,1)S(1)}, bf16[16,6144]{1,0:T(8,128)(2,1)}, u32[]{:S(2)}) copy-start(bf16[16,6144]{1,0:T(8,128)(2,1)} %param.18) | copy-start | bytes 589828
  79.5 16.2 %copy-start.5 = (f32[6144]{0:T(1024)S(1)}, f32[6144]{0:T(1024)}, u32[]{:S(2)}) copy-start(f32[6144]{0:T(1024)} %param.19) | copy-start | bytes 73732
  82.0 11.7 %all-to-all-start.1 = ((bf16[8,4,768]{2,1,0:T(4,128)(2,1)}), bf16[8,4,768]{2,1,0:T(4,128)(2,1)S(1)}, u32[]{:S(2)}, u32[]{:S(2)}) async-start(bf16[8,4,768]{2,1,0:T(4,128)(2,1)} %convert_element_type.30), calls=%async_computation.1 | async-start | bytes 98304 | tf_op jit(solution)/shard_map/all_to_all | solution.py:134
  87.4 178.1 %all-gather.12.cloned.1.call-start = ((), (), s32[]{:S(2)}) async-start(), calls=%async_computation.3 | async-start | bytes 26738688 | tf_op jit(solution)/shard_map/all_gather | solution.py:140
  87.7 32.1 %copy-start.6 = (s32[2048]{0:T(1024)S(1)}, s32[2048]{0:T(1024)}, u32[]{:S(2)}) copy-start(s32[2048]{0:T(1024)} %param.21) | copy-start | bytes 24580
Sparse Core Ops, SparseCore 0:
  120.0 145.5 all-gather.11
